TPU v7x, 32 devices: a whole 2x2x4 slice. The times are simulated.
32 devices in a mesh: node: 8 (over z, y), rep: 4 (over x, core).
Axes of the slice: x: 2, y: 2, z: 4, core: 2. Of those that a mesh axis runs over, the one named last changes fastest.
Arguments:
- tokens: bfloat16 [4096, 8192], P(('node', 'rep')), may hold values from -6 to 6
- norm_gain: float32 [8192], replicated, may hold values from 0.5 to 1.5
- key_cotangent: bfloat16 [4096, 512], P(('node', 'rep')), may hold values from -6 to 6
- secondary: bfloat16 [8192, 512], P('node'), may hold values from -0.0625 to 0.0625
- master: float32 [8192, 512], P(('node', 'rep')), may hold values from -0.0625 to 0.0625
- moment_first: float32 [4096, 1024], P(('node', 'rep')), may hold values from -0.09375 to 0.09375
- moment_second: float32 [4096, 1024], P(('node', 'rep')), may hold values from 6.1035156e-05 to 0.0009765625
- signs: int32 [1024], replicated, may hold values from 0 to 1
Outputs:
- keys: bfloat16 [4096, 512], P(('node', 'rep'))
- token_grad: bfloat16 [4096, 8192], P(('node', 'rep'))
- new_master: float32 [8192, 512], P(('node', 'rep'))
- new_first: float32 [4096, 1024], P(('node', 'rep'))
- new_second: float32 [4096, 1024], P(('node', 'rep'))
- new_secondary: bfloat16 [8192, 512], P('node')
All inputs are finite; a program needn't handle non-finite values.
Results may differ from a plain program's by a relative error of at most 0.0049.
Values may be sent and summed in bfloat16 or wider, within the bound.
A program may use at most 128 MiB of HBM per device.

v0:
```python
import math

import jax
import jax.numpy as jnp
from jax import lax
from jax.sharding import PartitionSpec as P

PAIR_GAP = 16


norm_eps = 1e-05
adam_eps = 1e-08
beta_first = 0.9
beta_second = 0.95
adam_steps = 10
learn_rate = 0.002
weight_decay = 0.1


def sylvester(extent):
    position = jnp.arange(extent, dtype=jnp.int32)
    parity = jnp.zeros((extent, extent), jnp.int32)
    for bit_place in range(extent.bit_length() - 1):
        parity = parity + (position[:, None] >> bit_place & 1) * (
            position[None, :] >> bit_place & 1
        )
    return (1 - 2 * (parity % 2)).astype(jnp.float32)


def shards(tokens, norm_gain, key_cotangent, secondary, master, moment_first, moment_second, signs):
    tok_rows, model_width = tokens.shape
    key_width = key_cotangent.shape[1]
    node_count = lax.axis_size("node")
    rep_count = lax.axis_size("rep")
    all_tokens = tok_rows * node_count * rep_count
    had_table = sylvester(key_width)
    sign_rows = (1 - 2 * signs).astype(jnp.float32).reshape(2, key_width)
    floats = tokens.astype(jnp.float32)
    inverse = lax.rsqrt(jnp.mean(floats * floats, axis=-1, keepdims=True) + norm_eps)
    normed = floats * inverse
    hidden = (normed * norm_gain).astype(jnp.bfloat16)
    columns = hidden
    keys = jnp.dot(
        columns,
        lax.all_gather(secondary, "node", axis=0, tiled=True),
        preferred_element_type=jnp.float32,
    ).astype(jnp.bfloat16)
    hidden_grad = lax.dot_general(
        key_cotangent,
        lax.all_gather(secondary, "node", axis=0, tiled=True),
        (((1,), (1,)), ((), ())),
        preferred_element_type=jnp.float32,
    )
    scaled = hidden_grad * norm_gain
    token_grad = (
        inverse * (scaled - normed * jnp.mean(scaled * normed, axis=-1, keepdims=True))
    ).astype(jnp.bfloat16)
    rot_scale = 1.0 / (math.sqrt(2 * key_width) * all_tokens)
    flipped = (key_cotangent[:, None, :] * sign_rows.astype(jnp.bfloat16)).reshape(
        2 * tok_rows, key_width
    )
    rotated = (
        jnp.dot(flipped, had_table.astype(jnp.bfloat16), preferred_element_type=jnp.float32)
        * rot_scale
    )
    rotated = rotated.astype(jnp.bfloat16).reshape(tok_rows, 2, key_width)
    shard_rows = model_width // (node_count * rep_count)
    source = (
        hidden.reshape(tok_rows, node_count, rep_count, shard_rows)
        .transpose(0, 2, 1, 3)
        .reshape(tok_rows, model_width)
    )
    amount = lax.axis_size("rep") * (model_width // 2 // rep_count)
    columns = source
    grouped = columns.reshape(tok_rows, amount // PAIR_GAP, 2, PAIR_GAP)
    halves = jnp.einsum("tgaj,tak->agjk", grouped, rotated, preferred_element_type=jnp.float32)
    joined = jnp.concatenate([halves[0] + halves[1], halves[0] - halves[1]], axis=-1)
    partial_sum = lax.psum_scatter(
        joined.reshape(amount, 2 * key_width).astype(jnp.bfloat16),
        "rep",
        scatter_dimension=0,
        tiled=True,
    )
    coded = lax.psum_scatter(partial_sum, "node", scatter_dimension=0, tiled=True).astype(
        jnp.float32
    )
    new_first = beta_first * moment_first + (1.0 - beta_first) * coded
    new_second = beta_second * moment_second + (1.0 - beta_second) * coded * coded
    first_hat = new_first / (1.0 - beta_first**adam_steps)
    second_hat = new_second / (1.0 - beta_second**adam_steps)
    ratio = first_hat / (jnp.sqrt(second_hat) + adam_eps)
    lower = ratio[:, :key_width]
    upper = ratio[:, key_width:]
    norm_root = math.sqrt(2 * key_width)
    row_even = (
        jnp.dot(lower + upper, had_table, precision=lax.Precision.HIGHEST)
        / norm_root
        * sign_rows[0]
    )
    row_odd = (
        jnp.dot(lower - upper, had_table, precision=lax.Precision.HIGHEST)
        / norm_root
        * sign_rows[1]
    )
    stacked = jnp.stack([row_even, row_odd], axis=1)
    master_rows = master.shape[0]
    update = (
        stacked.reshape(master_rows // (2 * PAIR_GAP), PAIR_GAP, 2, key_width)
        .transpose(0, 2, 1, 3)
        .reshape(master_rows, key_width)
    )
    new_master = master - learn_rate * (update + weight_decay * master)
    new_secondary = lax.all_gather(new_master.astype(jnp.bfloat16), "rep", axis=0, tiled=True)
    return (keys, token_grad, new_master, new_first, new_second, new_secondary)


def solution(mesh):
    return jax.shard_map(
        shards,
        mesh=mesh,
        in_specs=(
            P(("node", "rep"), None),
            P(),
            P(("node", "rep"), None),
            P("node", None),
            P(("node", "rep"), None),
            P(("node", "rep"), None),
            P(("node", "rep"), None),
            P(),
        ),
        out_specs=(
            P(("node", "rep"), None),
            P(("node", "rep"), None),
            P(("node", "rep"), None),
            P(("node", "rep"), None),
            P(("node", "rep"), None),
            P("node", None),
        ),
        check_vma=False,
    )
```

profile of v0, /device:TPU:0, one launch (start us, length us, event | category | flops | bytes accessed | tf_op | source)
XLA Modules:
  0.0 350.5 jit_solution(4079345351798301126)
XLA Ops:
  7.2 0.0 all-gather.3.cloned.1.call-start
  7.2 0.7 all-gather.3.cloned.1.call-update
  7.9 0.0 reduce-scatter.3.cloned.1.call-start
  7.9 0.7 subtract_convert_fusion.1
  8.7 1.2 broadcast_multiply_fusion
  9.8 0.1 mul.382
  10.0 0.0 copy-start
  10.0 0.0 copy-start.2
  10.0 0.0 copy-start.6
  10.0 1.4 fusion.11
  11.5 0.8 reshape.193
  12.3 0.0 copy-done
  12.3 0.5 fusion.8
  12.8 124.6 %all-gather.3.cloned.1.call-done = bf16[8192,512]{1,0:T(8,128)(2,1)} async-done(((bf16[1024,512]{1,0:T(8,128)(2,1)}), bf16[8192,512]{1,0:T(8,128)(2,1)}) %all-gather.3.cloned.1.call-update) | async-done | bytes 8388624 | tf_op jit(solution)/shard_map/all_gather | solution.py:45
  137.3 0.0 copy-done.2
  137.3 0.0 copy-done.6
  137.3 0.0 copy-start.1
  137.3 6.5 %fusion.4 = (f32[128]{0:T(128)S(1)}, f32[128,8192]{1,0:T(8,128)S(1)}) fusion(bf16[128,8192]{1,0:T(8,128)(2,1)S(1)} %copy-done, f32[128]{0:T(128)S(1)} %add_rsqrt_fusion, f32[8192]{0:T(1024)S(1)} %copy-done.6, bf16[128,512]{1,0:T(8,128)(2,1)S(1)} %copy-done.2, bf16[8192,512]{1,0:T(8,128)(2,1)} %all-gather.3.cloned.1.call-done), kind=kOutput, calls=%fused_computation.10 | convolution fusion | flops 1078984576 | bytes 14844928 | tf_op jit(solution)/shard_map/dot_general | solution.py:48
  143.8 0.0 copy-done.1
  143.8 2.6 fusion.7
  146.4 2.8 reshape.192
  149.2 4.5 %copy.16 = bf16[128,8,4,256]{0,3,1,2:T(8,128)(2,1)} copy(bf16[128,8,4,256]{3,2,1,0:T(4,128)(2,1)} %reshape.192) | data formatting | bytes 4194304 | tf_op jit(solution)/shard_map/reshape | solution.py:69
  153.7 3.9 %fusion.9 = f32[2,256,16,512]{3,1,2,0:T(8,128)S(1)} fusion(bf16[128,256,2,16]{0,3,2,1:T(8,128)(2,1)} %bitcast.24, bf16[128,2,512,1]{2,1,0,3:T(2,128)(2,1)} %bitcast.25), kind=kOutput, calls=%fused_computation.15 | convolution fusion | flops 1073741824 | bytes 19136512 | tf_op jit(solution)/shard_map/tgaj,tak->agjk/dot_general | solution.py:76
  157.7 2.7 add_convert_fusion
  160.4 4.3 %copy.19 = bf16[1,256,16,512]{3,2,1,0:T(8,128)(2,1)} copy(bf16[1,256,16,512]{3,1,2,0:T(8,128)(2,1)S(1)} %get-tuple-element.11) | data formatting | bytes 8388608 | tf_op jit(solution)/shard_map/convert.3
  164.7 4.3 %copy.20 = bf16[1,256,16,512]{3,2,1,0:T(8,128)(2,1)} copy(bf16[1,256,16,512]{3,1,2,0:T(8,128)(2,1)S(1)} %get-tuple-element.12) | data formatting | bytes 8388608 | tf_op jit(solution)/shard_map/convert.2
  169.0 7.9 %pad_maximum_fusion = bf16[4096,1024]{1,0:T(8,128)(2,1)} fusion(bf16[4096,512]{1,0:T(8,128)(2,1)} %bitcast.23, bf16[4096,512]{1,0:T(8,128)(2,1)} %bitcast.22), kind=kLoop, calls=%fused_computation.1 | loop fusion | flops 16777216 | bytes 16777216 | tf_op jit(solution)/shard_map/concatenate | solution.py:77
  176.9 0.0 copy-start.4
  176.9 0.0 copy-start.5
  176.9 0.0 reduce-scatter.3.cloned.1.call-update
  176.9 0.0 reduce-scatter.5.cloned.1.call-start
  177.0 69.7 %reduce-scatter.3.cloned.1.call-done = bf16[1024,1024]{1,0:T(8,128)(2,1)} async-done(((bf16[4096,1024]{1,0:T(8,128)(2,1)}), bf16[1024,1024]{1,0:T(8,128)(2,1)}) %reduce-scatter.3.cloned.1.call-update) | async-done | bytes 2097168 | tf_op jit(solution)/shard_map/reduce_scatter | solution.py:78
  246.7 0.0 reduce-scatter.5.cloned.1.call-update
  246.7 0.3 all-gather.5.cloned.1.call-start
  247.0 71.6 %reduce-scatter.5.cloned.1.call-done = bf16[128,1024]{1,0:T(8,128)(2,1)} async-done(((bf16[1024,1024]{1,0:T(8,128)(2,1)}), bf16[128,1024]{1,0:T(8,128)(2,1)}) %reduce-scatter.5.cloned.1.call-update) | async-done | bytes 262160 | tf_op jit(solution)/shard_map/reduce_scatter | solution.py:84
  318.6 0.0 copy-done.4
  318.6 0.0 copy-done.5
  318.6 2.3 add_divide_fusion
  320.8 1.9 convolution_multiply_fusion.3
  322.7 0.0 copy-start.3
  322.7 1.9 convolution_multiply_fusion.2
  324.7 0.0 copy-done.3
  324.7 1.0 fusion.41
  325.7 0.0 all-gather.5.cloned.1.call-update
  325.7 5.3 %convolution_convert_fusion = bf16[128,512]{1,0:T(8,128)(2,1)} fusion(bf16[128,8192]{1,0:T(8,128)(2,1)S(1)} %get-tuple-element.14, bf16[8192,512]{1,0:T(8,128)(2,1)} %all-gather.3.cloned.1.call-done), kind=kOutput, calls=%fused_computation.24 | convolution fusion | flops 1073807360 | bytes 10616832 | tf_op jit(solution)/shard_map/dot_general | solution.py:43
  331.1 10.6 %all-gather.5.cloned.1.call-done = bf16[1024,512]{1,0:T(8,128)(2,1)} async-done(((bf16[256,512]{1,0:T(8,128)(2,1)}), bf16[1024,512]{1,0:T(8,128)(2,1)}) %all-gather.5.cloned.1.call-update) | async-done | bytes 1048592 | tf_op jit(solution)/shard_map/all_gather | solution.py:113
  341.7 2.3 copy.30
  (11 shorter events, 0.1 us)
Async XLA Ops:
  7.2 130.2 %all-gather.3.cloned.1.call-start = ((), (), s32[]{:S(2)}) async-start(), calls=%async_computation.2 | async-start | bytes 9437184 | tf_op jit(solution)/shard_map/all_gather | solution.py:45
  7.9 238.8 %reduce-scatter.3.cloned.1.call-start = ((), (), s32[]{:S(2)}) async-start(), calls=%async_computation.3 | async-start | bytes 10485760 | tf_op jit(solution)/shard_map/reduce_scatter | solution.py:78
  10.0 2.3 copy-start
  10.0 127.3 %copy-start.2 = (bf16[128,512]{1,0:T(8,128)(2,1)S(1)}, bf16[128,512]{1,0:T(8,128)(2,1)}, u32[]{:S(2)}) copy-start(bf16[128,512]{1,0:T(8,128)(2,1)} %param.10) | copy-start | bytes 393220
  10.0 127.3 %copy-start.6 = (f32[8192]{0:T(1024)S(1)}, f32[8192]{0:T(1024)}, u32[]{:S(2)}) copy-start(f32[8192]{0:T(1024)} %param.9) | copy-start | bytes 98308
  137.3 6.5 %copy-start.1 = (bf16[128,8192]{1,0:T(8,128)(2,1)S(1)}, bf16[128,8192]{1,0:T(8,128)(2,1)}, u32[]{:S(2)}) copy-start(bf16[128,8192]{1,0:T(8,128)(2,1)} %param.8) | copy-start | bytes 6291460
  176.9 141.7 %copy-start.4 = (f32[128,1024]{1,0:T(8,128)S(1)}, f32[128,1024]{1,0:T(8,128)}, u32[]{:S(2)}) copy-start(f32[128,1024]{1,0:T(8,128)} %param.13) | copy-start | bytes 1572868
  176.9 141.7 %copy-start.5 = (f32[128,1024]{1,0:T(8,128)S(1)}, f32[128,1024]{1,0:T(8,128)}, u32[]{:S(2)}) copy-start(f32[128,1024]{1,0:T(8,128)} %param.14) | copy-start | bytes 1572868
  176.9 141.6 %reduce-scatter.5.cloned.1.call-start = ((), (), s32[]{:S(2)}) async-start(), calls=%async_computation.4 | async-start | bytes 2359296 | tf_op jit(solution)/shard_map/reduce_scatter | solution.py:84
  246.7 95.0 %all-gather.5.cloned.1.call-start = ((), (), s32[]{:S(2)}) async-start(), calls=%async_computation.5 | async-start | bytes 1310720 | tf_op jit(solution)/shard_map/all_gather | solution.py:113
  322.7 2.0 copy-start.3
Sparse Core Ops, SparseCore 0:
  10.1 127.1 all-gather.2
  177.0 69.5 reduce-scatter.2
  250.2 68.3 reduce-scatter.4
  325.9 15.7 all-gather.4
where the time goes:
time: 351 us; the launch traced here: 350 us
  waiting for transfers between devices  277 us (79%)
  matrix products  20.9 us (6%)
  local copies, waits for them, and re-layouts  19.2 us (5%)
  other arithmetic  18.9 us (5%)
  between operations  13.9 us (4%)
    all_gather x1, waiting for transfers between devices, shards(): lax.all_gather(secondary, 'node', axis=0, tiled=True)  125 us
    reduce_scatter x1, waiting for transfers between devices, shards(): lax.psum_scatter(partial_sum, 'node', scatter_dimension=0, tiled=True)  71.6 us
    reduce_scatter x1, waiting for transfers between devices, shards(): lax.psum_scatter(joined.reshape(amount, 2 * key_width).astype(jnp.bfloat1...  69.7 us
    all_gather x1, waiting for transfers between devices, shards(): lax.all_gather(new_master.astype(jnp.bfloat16), 'rep', axis=0, tiled=True)  10.6 us
    another operation x2, local copies, waits for them, and re-layouts  8.63 us
    concatenate x1, other arithmetic, shards(): jnp.concatenate([halves[0] + halves[1], halves[0] - halves[1]], axis=-1)  7.88 us
    reshape x2, local copies, waits for them, and re-layouts, shards(): hidden.reshape(tok_rows, node_count, rep_count, shard_rows)  7.34 us
  transfers between devices with their start and end apart: 4, of which 4 were waited for; matrix products, arithmetic and copies ran while one was open for 3% of the time, Pallas kernels for 0%

commit v1 on v0

v1 whole, which is shorter than its diff:
```python
import functools
import math

import jax
import jax.numpy as jnp
from jax import lax
from jax.experimental import pallas as pl
from jax.experimental.pallas import tpu as pltpu
from jax.sharding import PartitionSpec as P

PAIR_GAP = 16
MESH = pl.DeviceIdType.MESH

norm_eps = 1e-05
adam_eps = 1e-08
beta_first = 0.9
beta_second = 0.95
adam_steps = 10
learn_rate = 0.002
weight_decay = 0.1

ANY = pl.BlockSpec(memory_space=pl.ANY)
VMEM = pl.BlockSpec(memory_space=pltpu.VMEM)


def sylvester(extent):
    position = jnp.arange(extent, dtype=jnp.int32)
    parity = jnp.zeros((extent, extent), jnp.int32)
    for bit_place in range(extent.bit_length() - 1):
        parity = parity + (position[:, None] >> bit_place & 1) * (
            position[None, :] >> bit_place & 1
        )
    return (1 - 2 * (parity % 2)).astype(jnp.float32)


def split(index):
    return index // 2, lax.rem(index, 2)


def greet(peers):
    barrier = pltpu.get_barrier_semaphore()
    for peer in peers:
        pl.semaphore_signal(barrier, inc=1, device_id=peer, device_id_type=MESH)
    pl.semaphore_wait(barrier, len(peers))


def remote(src, dst, send, recv, peer):
    return pltpu.make_async_remote_copy(
        src_ref=src,
        dst_ref=dst,
        send_sem=send,
        recv_sem=recv,
        device_id=peer,
        device_id_type=MESH,
    )


def axis_peers(axis, size):
    me = lax.axis_index(axis)
    return [{axis: lax.rem(me + k, size)} for k in range(1, size)]


def pair_peers(axis, size):
    high, low = split(lax.axis_index(axis))
    half = size // 2
    partner = {axis: high * 2 + 1 - low}
    same = [{axis: lax.rem(high + k, half) * 2 + low} for k in range(1, half)]
    return partner, same


class PairGather:
    def __init__(self, axis, size, src, out, local_sem, send, recv):
        self.half = size // 2
        me = lax.axis_index(axis)
        high, low = split(me)
        partner, same = pair_peers(axis, size)
        self.local = pltpu.make_async_copy(src, out.at[me], local_sem)
        self.first = [
            remote(src, out.at[me], send.at[0, k], recv.at[0, k], same[k - 1])
            for k in range(1, self.half)
        ]
        self.second = [remote(src, out.at[me], send.at[1, 0], recv.at[1, 0], partner)]
        for k in range(1, self.half):
            origin = lax.rem(high + self.half - k, self.half) * 2 + low
            self.second.append(
                remote(out.at[origin], out.at[origin], send.at[1, k], recv.at[1, k], partner)
            )

    def start(self):
        for copy in self.first:
            copy.start()
        self.second[0].start()
        self.local.start()

    def forward(self):
        for arrived, onward in zip(self.first, self.second[1:]):
            arrived.wait_recv()
            onward.start()

    def finish(self):
        for copy in self.second:
            copy.wait_recv()
        for copy in self.first + self.second:
            copy.wait_send()
        self.local.wait()


def gather_kernel(
    nodes, reps, hid, cot, sec, hid_out, cot_out, sec_out, hs, hr, cs, cr, ss, sr, local
):
    rep = lax.axis_index("rep")
    partner, same = pair_peers("node", nodes)
    rep_peers = axis_peers("rep", reps)
    greet(rep_peers + [partner] + same)
    own = [
        pltpu.make_async_copy(hid.at[rep], hid_out.at[rep], local.at[0]),
        pltpu.make_async_copy(cot, cot_out.at[rep], local.at[1]),
    ]
    rows = sec_out.shape[1]
    weights = PairGather(
        "node", nodes, sec.at[pl.ds(pl.multiple_of(rep * rows, rows), rows)], sec_out,
        local.at[2], ss, sr,
    )
    weights.start()
    moves = []
    for k, peer in enumerate(rep_peers):
        moves.append(remote(cot, cot_out.at[rep], cs.at[k], cr.at[k], peer))
    for k, peer in enumerate(rep_peers):
        moves.append(remote(hid.at[peer["rep"]], hid_out.at[rep], hs.at[k], hr.at[k], peer))
    for copy in moves + own:
        copy.start()
    weights.forward()
    for copy in moves:
        copy.wait()
    weights.finish()
    for copy in own:
        copy.wait()


def gather(nodes, reps, hid, cot, sec):
    rows = sec.shape[0] // reps
    dma = pltpu.SemaphoreType.DMA
    return pl.pallas_call(
        functools.partial(gather_kernel, nodes, reps),
        out_shape=(
            jax.ShapeDtypeStruct(hid.shape, hid.dtype),
            jax.ShapeDtypeStruct((reps,) + cot.shape, cot.dtype),
            jax.ShapeDtypeStruct((nodes, rows, sec.shape[1]), sec.dtype),
        ),
        in_specs=[ANY] * 3,
        out_specs=(VMEM,) * 3,
        scratch_shapes=[dma((reps - 1,))] * 4 + [dma((2, nodes // 2))] * 2 + [dma((3,))],
        compiler_params=pltpu.CompilerParams(collective_id=0, has_side_effects=True),
    )(hid, cot, sec)


def reduce_kernel(
    nodes, reps, term, part, grad, coded, keys, grad_out,
    from_pair, to_same, from_same, key_in, ps, pr, zs, zr, ks, kr, gs, gr, local,
):
    rep = lax.axis_index("rep")
    high, low = split(lax.axis_index("node"))
    half = nodes // 2
    partner, same = pair_peers("node", nodes)
    rep_peers = axis_peers("rep", reps)
    greet(rep_peers + [partner] + same)
    f32 = jnp.float32
    pair = {}
    for k in list(range(1, half)) + [0]:
        there = lax.rem(high + k, half)
        pair[k] = remote(
            term.at[there * 2 + 1 - low], from_pair.at[k], ps.at[k], pr.at[k], partner
        )
        pair[k].start()
    swaps = []
    for k, peer in enumerate(rep_peers):
        swaps.append(remote(part.at[peer["rep"]], key_in.at[k], ks.at[k], kr.at[k], peer))
    for k, peer in enumerate(rep_peers):
        swaps.append(remote(grad.at[peer["rep"]], grad_out.at[rep], gs.at[k], gr.at[k], peer))
    own = pltpu.make_async_copy(grad.at[rep], grad_out.at[rep], local.at[0])
    for copy in swaps + [own]:
        copy.start()
    onward = []
    for k in range(1, half):
        there = lax.rem(high + k, half)
        pair[k].wait_recv()
        to_same[k - 1] = (
            term[there * 2 + low].astype(f32) + from_pair[k].astype(f32)
        ).astype(to_same.dtype)
        onward.append(
            remote(
                to_same.at[k - 1], from_same.at[k - 1], zs.at[k - 1], zr.at[k - 1], same[k - 1]
            )
        )
        onward[-1].start()
    pair[0].wait_recv()
    coded[...] = term[high * 2 + low].astype(f32) + from_pair[0].astype(f32)
    for k in range(reps - 1):
        swaps[k].wait_recv()
    total = part[rep].astype(f32)
    for k in range(reps - 1):
        total = total + key_in[k].astype(f32)
    keys[...] = total.astype(keys.dtype)
    for k in range(1, half):
        onward[k - 1].wait_recv()
        coded[...] += from_same[k - 1].astype(f32)
    for copy in swaps[reps - 1 :]:
        copy.wait_recv()
    for copy in swaps + onward + list(pair.values()):
        copy.wait_send()
    own.wait()


def reduce(nodes, reps, term, part, grad):
    dma = pltpu.SemaphoreType.DMA
    half = nodes // 2
    block = term.shape[1:]
    return pl.pallas_call(
        functools.partial(reduce_kernel, nodes, reps),
        out_shape=(
            jax.ShapeDtypeStruct(block, jnp.float32),
            jax.ShapeDtypeStruct(part.shape[1:], part.dtype),
            jax.ShapeDtypeStruct(grad.shape, grad.dtype),
        ),
        in_specs=[VMEM, VMEM, ANY],
        out_specs=(VMEM,) * 3,
        scratch_shapes=[
            pltpu.VMEM((half,) + block, term.dtype),
            pltpu.VMEM((half - 1,) + block, term.dtype),
            pltpu.VMEM((half - 1,) + block, term.dtype),
            pltpu.VMEM((reps - 1,) + part.shape[1:], part.dtype),
        ]
        + [dma((half,))] * 2
        + [dma((half - 1,))] * 2
        + [dma((reps - 1,))] * 4
        + [dma((1,))],
        compiler_params=pltpu.CompilerParams(collective_id=1, has_side_effects=True),
    )(term, part, grad)


def spread_kernel(reps, src, out, send, recv, local):
    partner, same = pair_peers("rep", reps)
    greet([partner] + same)
    rows = PairGather("rep", reps, src, out, local.at[0], send, recv)
    rows.start()
    rows.forward()
    rows.finish()


def spread(reps, rows):
    dma = pltpu.SemaphoreType.DMA
    return pl.pallas_call(
        functools.partial(spread_kernel, reps),
        out_shape=jax.ShapeDtypeStruct((reps,) + rows.shape, rows.dtype),
        in_specs=[VMEM],
        out_specs=VMEM,
        scratch_shapes=[dma((2, reps // 2))] * 2 + [dma((1,))],
        compiler_params=pltpu.CompilerParams(collective_id=2, has_side_effects=True),
    )(rows)


def shards(tokens, norm_gain, key_cotangent, secondary, master, moment_first, moment_second, signs):
    tok_rows, model_width = tokens.shape
    key_width = key_cotangent.shape[1]
    nodes = lax.axis_size("node")
    reps = lax.axis_size("rep")
    all_tokens = tok_rows * nodes * reps
    group_tokens = tok_rows * reps
    master_rows = master.shape[0]
    quarter = model_width // reps
    had_table = sylvester(key_width)
    sign_rows = (1 - 2 * signs).astype(jnp.float32).reshape(2, key_width)
    floats = tokens.astype(jnp.float32)
    inverse = lax.rsqrt(jnp.mean(floats * floats, axis=-1, keepdims=True) + norm_eps)
    normed = floats * inverse
    hidden = (normed * norm_gain).astype(jnp.bfloat16)
    outgoing = (
        hidden.reshape(tok_rows, nodes, reps, master_rows)
        .transpose(2, 0, 1, 3)
        .reshape(reps, tok_rows, quarter)
    )
    hid, cot, sec = gather(nodes, reps, outgoing, key_cotangent, secondary)
    hid = hid.reshape(group_tokens, quarter)
    cot = cot.reshape(group_tokens, key_width)
    sec = sec.reshape(quarter, key_width)
    rot_scale = 1.0 / (math.sqrt(2 * key_width) * all_tokens)
    table = (sign_rows[:, :, None] * had_table).astype(jnp.bfloat16)
    table = jnp.concatenate([table[0], table[1]], axis=1)
    rotated = (jnp.dot(cot, table, preferred_element_type=jnp.float32) * rot_scale).astype(
        jnp.bfloat16
    )
    products = lax.dot_general(
        hid, rotated, (((0,), (0,)), ((), ())), preferred_element_type=jnp.float32
    ).reshape(quarter // (2 * PAIR_GAP), 2, PAIR_GAP, 2 * key_width)
    upper_rows = products[:, 0, :, :key_width]
    lower_rows = products[:, 1, :, key_width:]
    term = jnp.concatenate([upper_rows + lower_rows, upper_rows - lower_rows], axis=-1)
    term = term.astype(jnp.bfloat16).reshape(nodes, master_rows // 2, 2 * key_width)
    part = jnp.dot(hid, sec, preferred_element_type=jnp.float32).astype(jnp.bfloat16)
    grad = lax.dot_general(
        cot, sec, (((1,), (1,)), ((), ())), preferred_element_type=jnp.float32
    ).astype(jnp.bfloat16)
    coded, keys, hidden_grad = reduce(
        nodes,
        reps,
        term,
        part.reshape(reps, tok_rows, key_width),
        grad.reshape(reps, tok_rows, quarter),
    )
    new_first = beta_first * moment_first + (1.0 - beta_first) * coded
    new_second = beta_second * moment_second + (1.0 - beta_second) * coded * coded
    first_hat = new_first / (1.0 - beta_first**adam_steps)
    second_hat = new_second / (1.0 - beta_second**adam_steps)
    ratio = first_hat / (jnp.sqrt(second_hat) + adam_eps)
    lower = ratio[:, :key_width]
    upper = ratio[:, key_width:]
    norm_root = math.sqrt(2 * key_width)
    row_even = (
        jnp.dot(lower + upper, had_table, precision=lax.Precision.HIGHEST)
        / norm_root
        * sign_rows[0]
    )
    row_odd = (
        jnp.dot(lower - upper, had_table, precision=lax.Precision.HIGHEST)
        / norm_root
        * sign_rows[1]
    )
    groups = master_rows // (2 * PAIR_GAP)
    update = jnp.stack(
        [
            row_even.reshape(groups, PAIR_GAP, key_width),
            row_odd.reshape(groups, PAIR_GAP, key_width),
        ],
        axis=1,
    ).reshape(master_rows, key_width)
    new_master = master - learn_rate * (update + weight_decay * master)
    new_secondary = spread(reps, new_master.astype(jnp.bfloat16)).reshape(
        reps * master_rows, key_width
    )
    hidden_grad = (
        hidden_grad.reshape(reps, tok_rows, nodes, master_rows)
        .transpose(1, 2, 0, 3)
        .reshape(tok_rows, model_width)
        .astype(jnp.float32)
    )
    scaled = hidden_grad * norm_gain
    token_grad = (
        inverse * (scaled - normed * jnp.mean(scaled * normed, axis=-1, keepdims=True))
    ).astype(jnp.bfloat16)
    return (keys, token_grad, new_master, new_first, new_second, new_secondary)


def solution(mesh):
    return jax.shard_map(
        shards,
        mesh=mesh,
        in_specs=(
            P(("node", "rep"), None),
            P(),
            P(("node", "rep"), None),
            P("node", None),
            P(("node", "rep"), None),
            P(("node", "rep"), None),
            P(("node", "rep"), None),
            P(),
        ),
        out_specs=(
            P(("node", "rep"), None),
            P(("node", "rep"), None),
            P(("node", "rep"), None),
            P(("node", "rep"), None),
            P(("node", "rep"), None),
            P("node", None),
        ),
        check_vma=False,
    )
```

time: 351 us -> 162 us (0.46)
  waiting for transfers between devices: 277 us -> 0 us
  Pallas kernels: 0 us -> 89.8 us
  between operations: 13.9 us -> 0.86 us
  local copies, waits for them, and re-layouts: 19.2 us -> 32.1 us
    reduce_scatter x2 -> x0, waiting for transfers between devices: 141 us -> none  [the longest x1 71.6 us: shards(): lax.psum_scatter(partial_sum, 'node', scatter_dimension=0, tiled=True)]
    all_gather x2 -> x0, waiting for transfers between devices: 135 us -> none  [the longest x1 125 us: shards(): lax.all_gather(secondary, 'node', axis=0, tiled=True)]
    pallas_call x0 -> x3, Pallas kernels: none -> 89.8 us  [the longest x1 39.2 us: reduce(): pl.pallas_call(functools.partial(reduce_kernel, nodes, reps), out_shape=(...]
    convert_element_type x1 -> x3, local copies, waits for them, and re-layouts: 0.01 us -> 10.8 us  [shards(): hidden_grad = hidden_grad.reshape(reps, tok_rows, nodes, master_rows).tra...]
    another operation x2 -> x0, local copies, waits for them, and re-layouts: 8.63 us -> none
    concatenate x1, other arithmetic: 7.88 us -> 1.58 us  [shards(): jnp.concatenate([upper_rows + lower_rows, upper_rows - lower_rows], axis=-1)]
    dot_general x0 -> x1, local copies, waits for them, and re-layouts: none -> 3.92 us  [shards(): lax.dot_general(hid, rotated, (((0,), (0,)), ((), ())), preferred_element...]
    reshape x3, local copies, waits for them, and re-layouts: 8.15 us -> 11.9 us  [the longest x2 7.7 us: shards(): hidden.reshape(tok_rows, nodes, reps, master_rows).transpose(2, 0, 1, 3)]
  transfers between devices with their start and end apart: 4 -> 0, of which waited for: 4 -> 0; matrix products, arithmetic and copies ran while one was open for 3% -> 0% of each run, Pallas kernels for 0% -> 0%
where the time goes in v1:
time: 162 us; the launch traced here: 160 us
  Pallas kernels  89.8 us (55%)
  local copies, waits for them, and re-layouts  32.1 us (20%)
  other arithmetic  18.8 us (12%)
  matrix products  18.6 us (11%)
    pallas_call x1, Pallas kernels, reduce(): pl.pallas_call(functools.partial(reduce_kernel, nodes, reps), out_shape=(...  39.2 us
    pallas_call x1, Pallas kernels, gather(): pl.pallas_call(functools.partial(gather_kernel, nodes, reps), out_shape=(...  39.1 us
    pallas_call x1, Pallas kernels, spread(): pl.pallas_call(functools.partial(spread_kernel, reps), out_shape=jax.Shap...  11.4 us
    convert_element_type x3, local copies, waits for them, and re-layouts, shards(): hidden_grad = hidden_grad.reshape(reps, tok_rows, nodes, master_rows).tra...  10.8 us
    dot_general x1, matrix products, shards(): lax.dot_general(hid, rotated, (((0,), (0,)), ((), ())), preferred_element...  7.8 us
    reshape x2, local copies, waits for them, and re-layouts, shards(): hidden.reshape(tok_rows, nodes, reps, master_rows).transpose(2, 0, 1, 3)  7.7 us
    unnamed x25, local copies, waits for them, and re-layouts  5.3 us
    dot_general x1, matrix products, shards(): jnp.dot(hid, sec, preferred_element_type=jnp.float32).astype(jnp.bfloat16)  4.42 us

profile of v1, /device:TPU:0, one launch (start us, length us, event | category | flops | bytes accessed | tf_op | source)
XLA Modules:
  0.0 160.2 jit_solution(8127356112047320524)
XLA Ops:
  0.6 0.0 copy-start.8
  0.6 2.1 %fusion.8 = f32[128]{0:T(128)S(1)} fusion(bf16[128,8192]{1,0:T(8,128)(2,1)} %param.8), kind=kLoop, calls=%fused_computation.10 | loop fusion | flops 3145600 | bytes 2097664 | tf_op jit(solution)/shard_map/reduce_sum | solution.py:274
  2.7 0.0 copy-done.8
  2.8 1.2 fusion.13
  4.0 0.0 copy-start.1
  4.0 0.0 copy-start.6
  4.0 0.2 multiply_convert_fusion.1
  4.3 0.1 slice_bitcast_fusion.1
  4.3 1.3 copy-done.1
  5.6 0.0 copy-done.6
  5.6 1.9 %fusion.3 = bf16[128,8192]{1,0:T(8,128)(2,1)} fusion(bf16[128,8192]{1,0:T(8,128)(2,1)S(1)} %copy-done.1, f32[8192]{0:T(1024)S(1)} %copy-done.6, f32[128]{0:T(128)S(1)} %add_rsqrt_fusion), kind=kLoop, calls=%fused_computation.5 | loop fusion | flops 4194304 | bytes 4227584 | tf_op jit(solution)/shard_map/convert_element_type | solution.py:276
  7.5 4.5 %reshape.468 = bf16[128,8,4,256]{3,2,1,0:T(4,128)(2,1)} reshape(bf16[128,8192]{1,0:T(8,128)(2,1)} %fusion.3) | data formatting | bytes 4194304 | tf_op jit(solution)/shard_map/reshape | solution.py:278
  12.0 3.2 %copy.22 = bf16[128,8,4,256]{3,1,0,2:T(8,128)(2,1)} copy(bf16[128,8,4,256]{3,2,1,0:T(4,128)(2,1)} %reshape.468) | data formatting | bytes 4194304 | tf_op jit(solution)/shard_map/reshape | solution.py:278
  15.2 4.2 %reshape.469.hid = bf16[4,128,2048]{2,1,0:T(8,128)(2,1)} reshape(bf16[4,128,8,256]{3,2,1,0:T(8,128)(2,1)} %bitcast.55) | data formatting | bytes 4194304 | tf_op jit(solution)/shard_map/reshape | solution.py:280
  19.4 39.1 %shard_map.127 = (bf16[4,128,2048]{2,1,0:T(8,128)(2,1)}, bf16[4,128,512]{2,1,0:T(8,128)(2,1)}, bf16[8,256,512]{2,1,0:T(8,128)(2,1)}) custom-call(bf16[4,128,2048]{2,1,0:T(8,128)(2,1)} %reshape.469.hid, bf16[128,512]{1,0:T(8,128)(2,1)} %cot.1, bf16[1024,512]{1,0:T(8,128)(2,1)} %sec.1), custom_call_target="tpu_custom_call" | custom-call | tf_op jit(solution)/shard_map/pallas_call | solution.py:143
  58.6 0.0 copy-start.9
  58.6 0.0 copy-start.10
  58.6 4.4 %convolution_convert_fusion.1 = bf16[512,512]{1,0:T(8,128)(2,1)} fusion(bf16[512,2048]{1,0:T(8,128)(2,1)} %bitcast.61, bf16[2048,512]{1,0:T(8,128)(2,1)} %bitcast.67), kind=kOutput, calls=%fused_computation.23 | convolution fusion | flops 1074003968 | bytes 4718592 | tf_op jit(solution)/shard_map/dot_general | solution.py:299
  63.0 0.0 copy-done.9
  63.0 0.0 copy-done.10
  63.0 2.7 %convolution_convert_fusion = bf16[512,2048]{1,0:T(8,128)(2,1)} fusion(bf16[512,512]{1,0:T(8,128)(2,1)S(1)} %bitcast.70, bf16[2048,512]{1,0:T(8,128)(2,1)S(1)} %bitcast.68), kind=kOutput, calls=%fused_computation.12 | convolution fusion | flops 1074790400 | bytes 4718592 | tf_op jit(solution)/shard_map/dot_general | solution.py:300
  65.7 3.9 %copy.15 = bf16[2048,512]{1,0:T(8,128)(2,1)} copy(bf16[2048,512]{0,1:T(8,128)(2,1)} %bitcast.62) | data formatting | bytes 4194304 | tf_op jit(solution)/shard_map/dot_general | solution.py:292
  69.6 7.8 %fusion.18 = f32[64,2,16,1024]{3,2,1,0:T(8,128)} fusion(bf16[64,2,16,512]{3,2,1,0:T(8,128)(2,1)} %bitcast.63, bf16[512,512]{1,0:T(8,128)(2,1)} %bitcast.69, bf16[512,512]{1,0:T(8,128)(2,1)S(1)} %get-tuple-element.26, bf16[512,512]{1,0:T(8,128)(2,1)S(1)} %get-tuple-element.25), kind=kOutput, calls=%fused_computation.33 | convolution fusion | flops 2687500288 | bytes 12058624 | tf_op jit(solution)/shard_map/dot_general | solution.py:292
  77.4 2.9 %add_convert_fusion = (bf16[64,1,16,512]{3,2,1,0:T(8,128)(2,1)S(1)}, bf16[64,1,16,512]{3,2,1,0:T(8,128)(2,1)S(1)}) fusion(f32[64,2,16,1024]{3,2,1,0:T(8,128)} %fusion.18), kind=kLoop, calls=%fused_computation.16 | loop fusion | flops 2097152 | bytes 6291456 | tf_op jit(solution)/shard_map/convert.6
  80.3 1.6 pad_maximum_fusion.term
  81.9 0.0 copy-start.4
  81.9 0.0 copy-start.5
  81.9 39.2 %shard_map.128 = (f32[128,1024]{1,0:T(8,128)}, bf16[128,512]{1,0:T(8,128)(2,1)}, bf16[4,128,2048]{2,1,0:T(8,128)(2,1)}) custom-call(bf16[8,128,1024]{2,1,0:T(8,128)(2,1)} %pad_maximum_fusion.term, bf16[4,128,512]{2,1,0:T(8,128)(2,1)} %bitcast.64, bf16[4,128,2048]{2,1,0:T(8,128)(2,1)} %bitcast.60), custom_call_target="tpu_custom_call" | custom-call | tf_op jit(solution)/shard_map/pallas_call | solution.py:218
  121.2 0.0 copy-done.4
  121.2 0.0 copy-done.5
  121.2 2.3 %add_divide_fusion = (f32[128,1024]{1,0:T(8,128)S(1)}, f32[128,1024]{1,0:T(8,128)}, f32[128,1024]{1,0:T(8,128)}) fusion(f32[128,1024]{1,0:T(8,128)} %get-tuple-element.17, f32[128,1024]{1,0:T(8,128)S(1)} %copy-done.4, f32[128,1024]{1,0:T(8,128)S(1)} %copy-done.5), kind=kLoop, calls=%fused_computation.42 | loop fusion | flops 1441792 | bytes 3145728 | tf_op jit(solution)/shard_map/div | solution.py:314
  123.5 1.9 %convolution_multiply_fusion.1 = f32[128,512]{1,0:T(8,128)S(1)} fusion(f32[128,1024]{1,0:T(8,128)S(1)} %get-tuple-element.20, f32[512]{0:T(512)S(1)} %get-tuple-element.27, s32[512]{0:T(512)S(1)} %get-tuple-element.29, s32[512]{0:T(512)S(1)} %get-tuple-element.30, s32[512]{0:T(512)S(1)} %get-tuple-element.31, s32[512]{0:T(512)S(1)} %get-tuple-element.32, ...), kind=kOutput, calls=%fused_computation.25 | convolution fusion | flops 410910720 | bytes 825344 | tf_op jit(solution)/shard_map/dot_general | solution.py:319
  125.4 0.0 copy-start.3
  125.4 1.9 %convolution_multiply_fusion = f32[128,512]{1,0:T(8,128)S(1)} fusion(f32[128,1024]{1,0:T(8,128)S(1)} %get-tuple-element.20, f32[512]{0:T(512)S(1)} %get-tuple-element.28, s32[512]{0:T(512)S(1)} %get-tuple-element.29, s32[512]{0:T(512)S(1)} %get-tuple-element.30, s32[512]{0:T(512)S(1)} %get-tuple-element.31, s32[512]{0:T(512)S(1)} %get-tuple-element.32, ...), kind=kOutput, calls=%fused_computation.24 | convolution fusion | flops 410910720 | bytes 825344 | tf_op jit(solution)/shard_map/dot_general | solution.py:324
  127.4 0.0 copy-done.3
  127.4 1.0 fusion.34
  128.4 11.4 %shard_map.129 = bf16[4,256,512]{2,1,0:T(8,128)(2,1)} custom-call(bf16[256,512]{1,0:T(8,128)(2,1)} %get-tuple-element.18.src), custom_call_target="tpu_custom_call" | custom-call | tf_op jit(solution)/shard_map/pallas_call | solution.py:252
  139.8 2.1 %copy.20 = f32[64,8,8,256]{3,2,1,0:T(8,128)S(1)} copy(bf16[64,8,8,256]{3,1,2,0:T(8,128)(2,1)} %bitcast.59) | data formatting | bytes 6291456
  141.9 0.3 bitcast_bitcast_fusion
  142.2 4.7 %copy.16 = f32[128,8,4,256]{3,2,1,0:T(4,128)} copy(f32[128,8,4,256]{3,1,0,2:T(8,128)S(1)} %bitcast_bitcast_fusion) | data formatting | bytes 8388608 | tf_op jit(solution)/shard_map/convert_element_type | solution.py:344
  146.9 5.8 %reshape.477 = f32[128,8192]{1,0:T(8,128)} reshape(f32[128,8,4,256]{3,2,1,0:T(4,128)} %copy.16) | data formatting | bytes 8388608 | tf_op jit(solution)/shard_map/convert_element_type | solution.py:344
  152.7 3.2 %fusion.4 = f32[128]{0:T(128)S(1)} fusion(bf16[128,8192]{1,0:T(8,128)(2,1)S(1)} %copy-done.1, f32[128,8192]{1,0:T(8,128)} %reshape.477, f32[8192]{0:T(1024)S(1)} %copy-done.6, f32[128]{0:T(128)S(1)} %add_rsqrt_fusion), kind=kLoop, calls=%fused_computation.6 | loop fusion | flops 5242752 | bytes 6325248 | tf_op jit(solution)/shard_map/reduce_sum | solution.py:348
  155.9 0.3 copy-done
  156.2 2.3 %fusion.7 = bf16[128,8192]{1,0:T(8,128)(2,1)} fusion(bf16[128,8192]{1,0:T(8,128)(2,1)S(1)} %copy-done.1, f32[128,8192]{1,0:T(8,128)S(1)} %copy-done, f32[128]{0:T(128)S(1)} %broadcast_multiply_fusion, f32[8192]{0:T(1024)S(1)} %copy-done.6, f32[128]{0:T(128)S(1)} %add_rsqrt_fusion), kind=kLoop, calls=%fused_computation.9 | loop fusion | flops 7340032 | bytes 8422400 | tf_op jit(solution)/shard_map/convert_element_type | solution.py:349
  158.5 0.0 copy-done.7
  158.5 0.7 copy.25
  159.2 0.0 copy-done.2
  159.2 1.0 copy.26
  (14 shorter events, 0.1 us)
Async XLA Ops:
  0.6 2.1 %copy-start.8 = (s32[1024]{0:T(1024)S(1)}, s32[1024]{0:T(1024)}, u32[]{:S(2)}) copy-start(s32[1024]{0:T(1024)} %param.15) | copy-start | bytes 12292
  4.0 1.6 copy-start.1
  4.0 1.6 copy-start.6
  58.6 4.4 %copy-start.9 = (bf16[8,256,512]{2,1,0:T(8,128)(2,1)S(1)}, bf16[8,256,512]{2,1,0:T(8,128)(2,1)}, u32[]{:S(2)}) copy-start(bf16[8,256,512]{2,1,0:T(8,128)(2,1)} %get-tuple-element.14) | copy-start | bytes 6291460
  58.6 4.4 %copy-start.10 = (bf16[4,128,512]{2,1,0:T(8,128)(2,1)S(1)}, bf16[4,128,512]{2,1,0:T(8,128)(2,1)}, u32[]{:S(2)}) copy-start(bf16[4,128,512]{2,1,0:T(8,128)(2,1)} %get-tuple-element.13) | copy-start | bytes 1572868
  81.9 39.2 %copy-start.4 = (f32[128,1024]{1,0:T(8,128)S(1)}, f32[128,1024]{1,0:T(8,128)}, u32[]{:S(2)}) copy-start(f32[128,1024]{1,0:T(8,128)} %param.13) | copy-start | bytes 1572868
  81.9 39.2 %copy-start.5 = (f32[128,1024]{1,0:T(8,128)S(1)}, f32[128,1024]{1,0:T(8,128)}, u32[]{:S(2)}) copy-start(f32[128,1024]{1,0:T(8,128)} %param.14) | copy-start | bytes 1572868
  125.4 2.0 %copy-start.3 = (f32[256,512]{1,0:T(8,128)S(1)}, f32[256,512]{1,0:T(8,128)}, u32[]{:S(2)}) copy-start(f32[256,512]{1,0:T(8,128)} %param.12) | copy-start | bytes 1572868
  152.7 3.4 %copy-start = (f32[128,8192]{1,0:T(8,128)S(1)}, f32[128,8192]{1,0:T(8,128)}, u32[]{:S(2)}) copy-start(f32[128,8192]{1,0:T(8,128)} %reshape.477) | copy-start | bytes 12582916
  156.2 2.3 %copy-start.7 = (bf16[128,512]{1,0:T(8,128)(2,1)S(1)}, bf16[128,512]{1,0:T(8,128)(2,1)}, u32[]{:S(2)}) copy-start(bf16[128,512]{1,0:T(8,128)(2,1)} %get-tuple-element.43) | copy-start | bytes 393220
  156.2 3.0 %copy-start.2 = (bf16[4,256,512]{2,1,0:T(8,128)(2,1)S(1)}, bf16[4,256,512]{2,1,0:T(8,128)(2,1)}, u32[]{:S(2)}) copy-start(bf16[4,256,512]{2,1,0:T(8,128)(2,1)} %shard_map.129) | copy-start | bytes 3145732

commit v2 on v1

v2 whole, which is shorter than its diff:
```python
import functools
import math

import jax
import jax.numpy as jnp
from jax import lax
from jax.experimental import pallas as pl
from jax.experimental.pallas import tpu as pltpu
from jax.sharding import PartitionSpec as P

PAIR_GAP = 16
MESH = pl.DeviceIdType.MESH

norm_eps = 1e-05
adam_eps = 1e-08
beta_first = 0.9
beta_second = 0.95
adam_steps = 10
learn_rate = 0.002
weight_decay = 0.1

ANY = pl.BlockSpec(memory_space=pl.ANY)
VMEM = pl.BlockSpec(memory_space=pltpu.VMEM)


def sylvester(extent):
    position = jnp.arange(extent, dtype=jnp.int32)
    parity = jnp.zeros((extent, extent), jnp.int32)
    for bit_place in range(extent.bit_length() - 1):
        parity = parity + (position[:, None] >> bit_place & 1) * (
            position[None, :] >> bit_place & 1
        )
    return (1 - 2 * (parity % 2)).astype(jnp.float32)


def split(index):
    return index // 2, lax.rem(index, 2)


def greet(peers):
    barrier = pltpu.get_barrier_semaphore()
    for peer in peers:
        pl.semaphore_signal(barrier, inc=1, device_id=peer, device_id_type=MESH)
    pl.semaphore_wait(barrier, len(peers))


def remote(src, dst, send, recv, peer):
    return pltpu.make_async_remote_copy(
        src_ref=src,
        dst_ref=dst,
        send_sem=send,
        recv_sem=recv,
        device_id=peer,
        device_id_type=MESH,
    )


def axis_peers(axis, size):
    me = lax.axis_index(axis)
    return [{axis: lax.rem(me + k, size)} for k in range(1, size)]


def pair_peers(axis, size):
    high, low = split(lax.axis_index(axis))
    half = size // 2
    partner = {axis: high * 2 + 1 - low}
    same = [{axis: lax.rem(high + k, half) * 2 + low} for k in range(1, half)]
    return partner, same


class PairGather:
    def __init__(self, axis, size, src, out, local_sem, send, recv):
        self.half = size // 2
        me = lax.axis_index(axis)
        high, low = split(me)
        partner, same = pair_peers(axis, size)
        self.local = pltpu.make_async_copy(src, out.at[me], local_sem)
        self.first = [
            remote(src, out.at[me], send.at[0, k], recv.at[0, k], same[k - 1])
            for k in range(1, self.half)
        ]
        self.second = [remote(src, out.at[me], send.at[1, 0], recv.at[1, 0], partner)]
        for k in range(1, self.half):
            origin = lax.rem(high + self.half - k, self.half) * 2 + low
            self.second.append(
                remote(out.at[origin], out.at[origin], send.at[1, k], recv.at[1, k], partner)
            )

    def start(self):
        for copy in self.first:
            copy.start()
        self.second[0].start()
        self.local.start()

    def forward(self, k):
        self.first[k - 1].wait_recv()
        self.second[k].start()

    def finish(self):
        for copy in self.second:
            copy.wait_recv()
        for copy in self.first + self.second:
            copy.wait_send()
        self.local.wait()


def step_kernel(
    nodes, reps, aligned, scale, hid, cot, sec, table, coded, keys, grad_out,
    hid_in, cot_in, sec_in, rot, term, grad, acc, part,
    from_pair, to_same, from_same, key_in,
    cs, cr, hs, hr, ss, sr, ps, pr, zs, zr, gs, gr, ks, kr, cot_own, hid_own, sec_own, grad_own,
):
    f32 = jnp.float32
    rep = lax.axis_index("rep")
    high, low = split(lax.axis_index("node"))
    half = nodes // 2
    partner, same = pair_peers("node", nodes)
    rep_peers = axis_peers("rep", reps)
    columns, key_width = sec_in.shape[1:]
    tok_rows = cot_in.shape[1]
    group_tokens = reps * tok_rows

    def piece(ref, node, owner):
        index = node * reps + owner
        if aligned:
            return ref.at[:, pl.ds(pl.multiple_of(index * columns, columns), columns)]
        return ref.at[index]

    greet(rep_peers + [partner] + same)
    weights = PairGather(
        "node", nodes, sec.at[pl.ds(pl.multiple_of(rep * columns, columns), columns)], sec_in,
        sec_own.at[0], ss, sr,
    )
    weights.start()
    cot_moves = [
        remote(cot, cot_in.at[rep], cs.at[k], cr.at[k], peer) for k, peer in enumerate(rep_peers)
    ]
    cot_moves.append(pltpu.make_async_copy(cot, cot_in.at[rep], cot_own.at[0]))
    for copy in cot_moves:
        copy.start()
    turns = list(range(1, half)) + [0]
    order = [lax.rem(high + k, half) * 2 + 1 - low for k in turns]
    order += [lax.rem(high + k, half) * 2 + low for k in turns]
    hid_moves = []
    for i, node in enumerate(order):
        moves = [
            remote(
                piece(hid, node, peer["rep"]), hid_in.at[node, rep], hs.at[k, i], hr.at[k, i], peer
            )
            for k, peer in enumerate(rep_peers)
        ]
        moves.append(
            pltpu.make_async_copy(piece(hid, node, rep), hid_in.at[node, rep], hid_own.at[i])
        )
        for copy in moves:
            copy.start()
        hid_moves.append(moves)

    for copy in cot_moves:
        copy.wait()
    group_cot = cot_in[...].reshape(group_tokens, key_width)
    rot[...] = (jnp.dot(group_cot, table[...], preferred_element_type=f32) * scale).astype(
        rot.dtype
    )
    acc[...] = jnp.zeros_like(acc)

    def make_term(i):
        for copy in hid_moves[i]:
            copy.wait()
        chunk = hid_in[order[i]].reshape(group_tokens, columns)
        product = lax.dot_general(
            chunk, rot[...], (((0,), (0,)), ((), ())), preferred_element_type=f32
        ).reshape(columns // (2 * PAIR_GAP), 2, PAIR_GAP, 2 * key_width)
        first = product[:, 0, :, :key_width].reshape(columns // 2, key_width)
        second = product[:, 1, :, key_width:].reshape(columns // 2, key_width)
        term[i, :, :key_width] = (first + second).astype(term.dtype)
        term[i, :, key_width:] = (first - second).astype(term.dtype)

    swaps = []
    stays = []

    def use_weights(count, node):
        block = sec_in[node]
        rows = lax.dot_general(
            cot_in[...].reshape(group_tokens, key_width), block, (((1,), (1,)), ((), ())),
            preferred_element_type=f32,
        )
        grad[node] = rows.astype(grad.dtype).reshape(reps, tok_rows, columns)
        for k, peer in enumerate(rep_peers):
            copy = remote(
                grad.at[node, peer["rep"]], piece(grad_out, node, rep),
                gs.at[k, count], gr.at[k, count], peer,
            )
            copy.start()
            swaps.append(copy)
        copy = pltpu.make_async_copy(
            grad.at[node, rep], piece(grad_out, node, rep), grad_own.at[count]
        )
        copy.start()
        stays.append(copy)
        chunk = hid_in[node].reshape(group_tokens, columns)
        acc[...] += jnp.dot(chunk, block, preferred_element_type=f32)

    pairs = []
    for i in range(half):
        make_term(i)
        pairs.append(remote(term.at[i], from_pair.at[i], ps.at[i], pr.at[i], partner))
        pairs[-1].start()
        if i:
            weights.forward(i)
    weights.local.wait()
    onward = []
    for j, k in enumerate(turns):
        make_term(half + j)
        pairs[j].wait_recv()
        total = term[half + j].astype(f32) + from_pair[j].astype(f32)
        if k:
            to_same[j] = total.astype(to_same.dtype)
            onward.append(remote(to_same.at[j], from_same.at[j], zs.at[j], zr.at[j], same[k - 1]))
            onward[-1].start()
        else:
            coded[...] = total
        use_weights(j, order[half + j])
    for j in range(half):
        weights.second[j].wait_recv()
        use_weights(half + j, lax.rem(high + half - j, half) * 2 + 1 - low)
    part[...] = acc[...].astype(part.dtype).reshape(part.shape)
    key_moves = [
        remote(part.at[peer["rep"]], key_in.at[k], ks.at[k], kr.at[k], peer)
        for k, peer in enumerate(rep_peers)
    ]
    for copy in key_moves:
        copy.start()
    for j, copy in enumerate(onward):
        copy.wait_recv()
        coded[...] += from_same[j].astype(f32)
    total = part[rep].astype(f32)
    for k, copy in enumerate(key_moves):
        copy.wait_recv()
        total = total + key_in[k].astype(f32)
    keys[...] = total.astype(keys.dtype)
    for copy in swaps:
        copy.wait()
    for copy in stays:
        copy.wait()
    for copy in weights.first + weights.second + pairs + onward + key_moves:
        copy.wait_send()


def step(nodes, reps, aligned, scale, hid, cot, sec, table):
    dma = pltpu.SemaphoreType.DMA
    half = nodes // 2
    columns = sec.shape[0] // reps
    tok_rows, key_width = cot.shape
    group_tokens = reps * tok_rows
    block = (columns // 2, 2 * key_width)
    bf16 = jnp.bfloat16
    return pl.pallas_call(
        functools.partial(step_kernel, nodes, reps, aligned, scale),
        out_shape=(
            jax.ShapeDtypeStruct(block, jnp.float32),
            jax.ShapeDtypeStruct(cot.shape, bf16),
            jax.ShapeDtypeStruct(hid.shape, bf16),
        ),
        in_specs=[ANY, ANY, ANY, VMEM],
        out_specs=(VMEM,) * 3,
        scratch_shapes=[
            pltpu.VMEM((nodes, reps, tok_rows, columns), bf16),
            pltpu.VMEM((reps, tok_rows, key_width), bf16),
            pltpu.VMEM((nodes, columns, key_width), bf16),
            pltpu.VMEM((group_tokens, 2 * key_width), bf16),
            pltpu.VMEM((nodes,) + block, bf16),
            pltpu.VMEM((nodes, reps, tok_rows, columns), bf16),
            pltpu.VMEM((group_tokens, key_width), jnp.float32),
            pltpu.VMEM((reps, tok_rows, key_width), bf16),
            pltpu.VMEM((half,) + block, bf16),
            pltpu.VMEM((half - 1,) + block, bf16),
            pltpu.VMEM((half - 1,) + block, bf16),
            pltpu.VMEM((reps - 1, tok_rows, key_width), bf16),
        ]
        + [dma((reps - 1,))] * 2
        + [dma((reps - 1, nodes))] * 2
        + [dma((2, half))] * 2
        + [dma((half,))] * 2
        + [dma((half - 1,))] * 2
        + [dma((reps - 1, nodes))] * 2
        + [dma((reps - 1,))] * 2
        + [dma((1,)), dma((nodes,)), dma((1,)), dma((nodes,))],
        compiler_params=pltpu.CompilerParams(collective_id=0, has_side_effects=True),
    )(hid, cot, sec, table)


def spread_kernel(reps, src, out, send, recv, local):
    partner, same = pair_peers("rep", reps)
    greet([partner] + same)
    rows = PairGather("rep", reps, src, out, local.at[0], send, recv)
    rows.start()
    for k in range(1, reps // 2):
        rows.forward(k)
    rows.finish()


def spread(reps, rows):
    dma = pltpu.SemaphoreType.DMA
    return pl.pallas_call(
        functools.partial(spread_kernel, reps),
        out_shape=jax.ShapeDtypeStruct((reps,) + rows.shape, rows.dtype),
        in_specs=[VMEM],
        out_specs=VMEM,
        scratch_shapes=[dma((2, reps // 2))] * 2 + [dma((1,))],
        compiler_params=pltpu.CompilerParams(collective_id=1, has_side_effects=True),
    )(rows)


def shards(tokens, norm_gain, key_cotangent, secondary, master, moment_first, moment_second, signs):
    tok_rows, model_width = tokens.shape
    key_width = key_cotangent.shape[1]
    nodes = lax.axis_size("node")
    reps = lax.axis_size("rep")
    all_tokens = tok_rows * nodes * reps
    master_rows = master.shape[0]
    had_table = sylvester(key_width)
    sign_rows = (1 - 2 * signs).astype(jnp.float32).reshape(2, key_width)
    floats = tokens.astype(jnp.float32)
    inverse = lax.rsqrt(jnp.mean(floats * floats, axis=-1, keepdims=True) + norm_eps)
    normed = floats * inverse
    hidden = (normed * norm_gain).astype(jnp.bfloat16)
    aligned = master_rows % 128 == 0
    if not aligned:
        hidden = hidden.reshape(tok_rows, nodes * reps, master_rows).transpose(1, 0, 2)
    rot_scale = 1.0 / (math.sqrt(2 * key_width) * all_tokens)
    table = (had_table[:, None, :] * sign_rows.T[:, :, None]).astype(jnp.bfloat16)
    coded, keys, hidden_grad = step(
        nodes, reps, aligned, rot_scale, hidden, key_cotangent, secondary,
        table.reshape(key_width, 2 * key_width),
    )
    if not aligned:
        hidden_grad = hidden_grad.transpose(1, 0, 2).reshape(tok_rows, model_width)
    hidden_grad = hidden_grad.astype(jnp.float32)
    new_first = beta_first * moment_first + (1.0 - beta_first) * coded
    new_second = beta_second * moment_second + (1.0 - beta_second) * coded * coded
    first_hat = new_first / (1.0 - beta_first**adam_steps)
    second_hat = new_second / (1.0 - beta_second**adam_steps)
    ratio = first_hat / (jnp.sqrt(second_hat) + adam_eps)
    lower = ratio[:, :key_width]
    upper = ratio[:, key_width:]
    norm_root = math.sqrt(2 * key_width)
    row_even = (
        jnp.dot(lower + upper, had_table, precision=lax.Precision.HIGHEST)
        / norm_root
        * sign_rows[0]
    )
    row_odd = (
        jnp.dot(lower - upper, had_table, precision=lax.Precision.HIGHEST)
        / norm_root
        * sign_rows[1]
    )
    groups = master_rows // (2 * PAIR_GAP)
    update = jnp.stack(
        [
            row_even.reshape(groups, PAIR_GAP, key_width),
            row_odd.reshape(groups, PAIR_GAP, key_width),
        ],
        axis=1,
    ).reshape(master_rows, key_width)
    new_master = master - learn_rate * (update + weight_decay * master)
    new_secondary = spread(reps, new_master.astype(jnp.bfloat16)).reshape(
        reps * master_rows, key_width
    )
    scaled = hidden_grad * norm_gain
    token_grad = (
        inverse * (scaled - normed * jnp.mean(scaled * normed, axis=-1, keepdims=True))
    ).astype(jnp.bfloat16)
    return (keys, token_grad, new_master, new_first, new_second, new_secondary)


def solution(mesh):
    return jax.shard_map(
        shards,
        mesh=mesh,
        in_specs=(
            P(("node", "rep"), None),
            P(),
            P(("node", "rep"), None),
            P("node", None),
            P(("node", "rep"), None),
            P(("node", "rep"), None),
            P(("node", "rep"), None),
            P(),
        ),
        out_specs=(
            P(("node", "rep"), None),
            P(("node", "rep"), None),
            P(("node", "rep"), None),
            P(("node", "rep"), None),
            P(("node", "rep"), None),
            P("node", None),
        ),
        check_vma=False,
    )
```

time: 162 us -> 113 us (0.70)
  local copies, waits for them, and re-layouts: 32.1 us -> 4.34 us
  matrix products: 18.6 us -> 3.77 us
  other arithmetic: 18.8 us -> 13.6 us
    dot_general x3 -> x0, matrix products: 14.9 us -> none  [the longest x1 7.8 us: shards(): lax.dot_general(hid, rotated, (((0,), (0,)), ((), ())), preferred_element...]
    reshape x3 -> x1, local copies, waits for them, and re-layouts: 11.9 us -> 0.01 us  [shards(): sign_rows = (1 - 2 * signs).astype(jnp.float32).reshape(2, key_width)]
    convert_element_type x3 -> x0, local copies, waits for them, and re-layouts: 10.8 us -> none  [shards(): hidden_grad = hidden_grad.reshape(reps, tok_rows, nodes, master_rows).tra...]
    dot_general x1 -> x0, local copies, waits for them, and re-layouts: 3.92 us -> none  [shards(): lax.dot_general(hid, rotated, (((0,), (0,)), ((), ())), preferred_element...]
    another operation x1 -> x0, other arithmetic: 2.93 us -> none
    pallas_call x2 -> x1, Pallas kernels: 78.4 us -> 76.6 us  [step(): pl.pallas_call(functools.partial(step_kernel, nodes, reps, aligned, scale...]
    unnamed x25 -> x21, local copies, waits for them, and re-layouts: 5.3 us -> 4.19 us
where the time goes in v2:
time: 113 us; the launch traced here: 112 us
  Pallas kernels  89.6 us (79%)
  other arithmetic  13.6 us (12%)
  local copies, waits for them, and re-layouts  4.34 us (4%)
  matrix products  3.77 us (3%)
    pallas_call x1, Pallas kernels, step(): pl.pallas_call(functools.partial(step_kernel, nodes, reps, aligned, scale...  76.6 us
    pallas_call x1, Pallas kernels, spread(): pl.pallas_call(functools.partial(spread_kernel, reps), out_shape=jax.Shap...  13 us
    unnamed x21, local copies, waits for them, and re-layouts  4.19 us
    reduce_sum x1, other arithmetic, shards(): jnp.mean(scaled * normed, axis=-1, keepdims=True)  2.7 us
    convert_element_type x1, other arithmetic, shards(): token_grad = (inverse * (scaled - normed * jnp.mean(scaled * normed, axis...  2.39 us

profile of v2, /device:TPU:0, one launch (start us, length us, event | category | flops | bytes accessed | tf_op | source)
XLA Modules:
  0.0 112.2 jit_solution(12795050256716216053)
XLA Ops:
  0.6 0.0 copy-start.8
  0.6 2.1 %fusion.8 = f32[128]{0:T(128)S(1)} fusion(bf16[128,8192]{1,0:T(8,128)(2,1)} %param.8), kind=kLoop, calls=%fused_computation.10 | loop fusion | flops 3145600 | bytes 2097664 | tf_op jit(solution)/shard_map/reduce_sum | solution.py:325
  2.7 0.0 copy-done.8
  2.8 0.1 copy.16
  3.0 1.2 %fusion.12 = f32[512,512]{1,0:T(8,128)S(1)} fusion(s32[512]{0:T(512)S(1)} %get-tuple-element.19, s32[512]{0:T(512)S(1)} %get-tuple-element.20, s32[512]{0:T(512)S(1)} %get-tuple-element.21, s32[512]{0:T(512)S(1)} %get-tuple-element.22, s32[512]{0:T(512)S(1)} %get-tuple-element.23, s32[512]{0:T(512)S(1)} %get-tuple-element.24, s32[512]{0:T(512)S(1)} %get-tuple-element.25, ...), kind=kLoop, calls=%fused_computation.21 | loop fusion | flops 8126464 | bytes 1067008 | tf_op jit(solution)/shard_map/convert_element_type | solution.py:33
  4.2 0.0 copy-start
  4.2 0.0 copy-start.6
  4.2 1.0 multiply_convert_fusion
  5.2 1.2 %copy.19 = bf16[64,8,2,512]{3,1,2,0:T(8,128)(2,1)} copy(bf16[64,8,2,512]{3,2,1,0:T(2,128)(2,1)S(1)} %bitcast.18) | data formatting | bytes 2097152
  6.4 0.0 copy-done
  6.4 0.0 copy-done.6
  6.4 1.9 %fusion.3.hid = bf16[128,8192]{1,0:T(8,128)(2,1)} fusion(bf16[128,8192]{1,0:T(8,128)(2,1)S(1)} %copy-done, f32[8192]{0:T(1024)S(1)} %copy-done.6, f32[128]{0:T(128)S(1)} %add_rsqrt_fusion), kind=kLoop, calls=%fused_computation.5 | loop fusion | flops 4194304 | bytes 4227584 | tf_op jit(solution)/shard_map/convert_element_type | solution.py:327
  8.3 76.6 %shard_map.127 = (f32[128,1024]{1,0:T(8,128)}, bf16[128,512]{1,0:T(8,128)(2,1)}, bf16[128,8192]{1,0:T(8,128)(2,1)}) custom-call(bf16[128,8192]{1,0:T(8,128)(2,1)} %fusion.3.hid, bf16[128,512]{1,0:T(8,128)(2,1)} %cot.1, bf16[1024,512]{1,0:T(8,128)(2,1)} %sec.1, bf16[512,1024]{1,0:T(8,128)(2,1)} %bitcast.19), custom_call_target="tpu_custom_call" | custom-call | tf_op jit(solution)/shard_map/pallas_call | solution.py:258
  85.0 0.0 copy-start.1
  85.0 2.7 %fusion.4 = f32[128]{0:T(128)S(1)} fusion(bf16[128,8192]{1,0:T(8,128)(2,1)S(1)} %copy-done, bf16[128,8192]{1,0:T(8,128)(2,1)} %get-tuple-element.10, f32[8192]{0:T(1024)S(1)} %copy-done.6, f32[128]{0:T(128)S(1)} %add_rsqrt_fusion), kind=kLoop, calls=%fused_computation.6 | loop fusion | flops 6291328 | bytes 4228096 | tf_op jit(solution)/shard_map/reduce_sum | solution.py:372
  87.7 0.0 copy-done.1
  87.7 0.0 copy-start.3
  87.7 0.0 copy-start.4
  87.7 0.0 copy-start.5
  87.7 2.4 %fusion.7 = bf16[128,8192]{1,0:T(8,128)(2,1)} fusion(bf16[128,8192]{1,0:T(8,128)(2,1)S(1)} %copy-done, bf16[128,8192]{1,0:T(8,128)(2,1)S(1)} %copy-done.1, f32[128]{0:T(128)S(1)} %broadcast_multiply_fusion, f32[8192]{0:T(1024)S(1)} %copy-done.6, f32[128]{0:T(128)S(1)} %add_rsqrt_fusion), kind=kLoop, calls=%fused_computation.9 | loop fusion | flops 8388608 | bytes 6325248 | tf_op jit(solution)/shard_map/convert_element_type | solution.py:373
  90.1 0.0 copy-done.3
  90.1 0.0 copy-done.4
  90.1 0.0 copy-done.5
  90.1 1.3 %add_divide_fusion = (f32[128,1024]{1,0:T(8,128)S(1)}, f32[128,1024]{1,0:T(8,128)}, f32[128,1024]{1,0:T(8,128)}) fusion(f32[128,1024]{1,0:T(8,128)S(1)} %copy-done.5, f32[128,1024]{1,0:T(8,128)S(1)} %copy-done.3, f32[128,1024]{1,0:T(8,128)S(1)} %copy-done.4), kind=kLoop, calls=%fused_computation.28 | loop fusion | flops 1441792 | bytes 3145728 | tf_op jit(solution)/shard_map/div | solution.py:344
  91.4 1.9 %convolution_multiply_fusion.1 = f32[128,512]{1,0:T(8,128)S(1)} fusion(f32[128,1024]{1,0:T(8,128)S(1)} %get-tuple-element.14, f32[512]{0:T(512)S(1)} %get-tuple-element.17, s32[512]{0:T(512)S(1)} %get-tuple-element.19, s32[512]{0:T(512)S(1)} %get-tuple-element.20, s32[512]{0:T(512)S(1)} %get-tuple-element.21, s32[512]{0:T(512)S(1)} %get-tuple-element.22, ...), kind=kOutput, calls=%fused_computation.17 | convolution fusion | flops 410910720 | bytes 825344 | tf_op jit(solution)/shard_map/dot_general | solution.py:349
  93.3 0.0 copy-start.2
  93.3 1.9 %convolution_multiply_fusion = f32[128,512]{1,0:T(8,128)S(1)} fusion(f32[128,1024]{1,0:T(8,128)S(1)} %get-tuple-element.14, f32[512]{0:T(512)S(1)} %get-tuple-element.18, s32[512]{0:T(512)S(1)} %get-tuple-element.19, s32[512]{0:T(512)S(1)} %get-tuple-element.20, s32[512]{0:T(512)S(1)} %get-tuple-element.21, s32[512]{0:T(512)S(1)} %get-tuple-element.22, ...), kind=kOutput, calls=%fused_computation.16 | convolution fusion | flops 410910720 | bytes 825344 | tf_op jit(solution)/shard_map/dot_general | solution.py:354
  95.2 0.0 copy-start.7
  95.3 0.0 copy-done.2
  95.3 1.0 fusion.24
  96.3 13.0 %shard_map.128 = bf16[4,256,512]{2,1,0:T(8,128)(2,1)} custom-call(bf16[256,512]{1,0:T(8,128)(2,1)} %get-tuple-element.12.src), custom_call_target="tpu_custom_call" | custom-call | tf_op jit(solution)/shard_map/pallas_call | solution.py:305
  109.3 0.0 copy-done.7
  109.3 0.7 copy.22
  110.0 2.3 %copy.23 = bf16[1024,512]{1,0:T(8,128)(2,1)} copy(bf16[1024,512]{1,0:T(8,128)(2,1)} %bitcast.17) | data formatting | bytes 2097152
  (11 shorter events, 0.1 us)
Async XLA Ops:
  0.6 2.1 %copy-start.8 = (s32[1024]{0:T(1024)S(1)}, s32[1024]{0:T(1024)}, u32[]{:S(2)}) copy-start(s32[1024]{0:T(1024)} %param.15) | copy-start | bytes 12292
  4.2 2.3 %copy-start = (bf16[128,8192]{1,0:T(8,128)(2,1)S(1)}, bf16[128,8192]{1,0:T(8,128)(2,1)}, u32[]{:S(2)}) copy-start(bf16[128,8192]{1,0:T(8,128)(2,1)} %param.8) | copy-start | bytes 6291460
  4.2 2.3 %copy-start.6 = (f32[8192]{0:T(1024)S(1)}, f32[8192]{0:T(1024)}, u32[]{:S(2)}) copy-start(f32[8192]{0:T(1024)} %param.9) | copy-start | bytes 98308
  85.0 2.7 %copy-start.1 = (bf16[128,8192]{1,0:T(8,128)(2,1)S(1)}, bf16[128,8192]{1,0:T(8,128)(2,1)}, u32[]{:S(2)}) copy-start(bf16[128,8192]{1,0:T(8,128)(2,1)} %get-tuple-element.10) | copy-start | bytes 6291460
  87.7 2.4 %copy-start.3 = (f32[128,1024]{1,0:T(8,128)S(1)}, f32[128,1024]{1,0:T(8,128)}, u32[]{:S(2)}) copy-start(f32[128,1024]{1,0:T(8,128)} %param.13) | copy-start | bytes 1572868
  87.7 2.4 %copy-start.4 = (f32[128,1024]{1,0:T(8,128)S(1)}, f32[128,1024]{1,0:T(8,128)}, u32[]{:S(2)}) copy-start(f32[128,1024]{1,0:T(8,128)} %param.14) | copy-start | bytes 1572868
  87.7 2.4 %copy-start.5 = (f32[128,1024]{1,0:T(8,128)S(1)}, f32[128,1024]{1,0:T(8,128)}, u32[]{:S(2)}) copy-start(f32[128,1024]{1,0:T(8,128)} %get-tuple-element.11) | copy-start | bytes 1572868
  93.3 2.0 %copy-start.2 = (f32[256,512]{1,0:T(8,128)S(1)}, f32[256,512]{1,0:T(8,128)}, u32[]{:S(2)}) copy-start(f32[256,512]{1,0:T(8,128)} %param.12) | copy-start | bytes 1572868
  95.2 14.1 %copy-start.7 = (bf16[128,512]{1,0:T(8,128)(2,1)S(1)}, bf16[128,512]{1,0:T(8,128)(2,1)}, u32[]{:S(2)}) copy-start(bf16[128,512]{1,0:T(8,128)(2,1)} %get-tuple-element.33) | copy-start | bytes 393220
